TPU v7x, 128 devices: a whole 4x4x4 slice. The times are simulated.
128 devices in a mesh: rows: 8 (over z, core), cols: 16 (over x, y).
Axes of the slice: x: 4, y: 4, z: 4, core: 2. Of those that a mesh axis runs over, the one named last changes fastest.
Arguments:
- pixels: bfloat16 [3, 1024, 4096], P(None, 'rows', 'cols'), may hold values from -6 to 6
- patch_weight: bfloat16 [48, 256], replicated, may hold values from -0.875 to 0.875
- patch_bias: float32 [256], replicated, may hold values from -4 to 4
- conv_kernel: float32 [49, 256], replicated, may hold values from -0.875 to 0.875
- norm_gain: float32 [256], replicated, may hold values from 0.1 to 1.9
- kv_weight: bfloat16 [256, 2048], replicated, may hold values from -0.375 to 0.375
- latents: bfloat16 [256, 1024], replicated, may hold values from -80 to 80, as said below
- d_attended: bfloat16 [256, 1024], replicated, may hold values from -6 to 6
Outputs:
- attended: float32 [256, 1024], replicated
- grad_latents: float32 [256, 1024], replicated
- grad_kv_weight: float32 [256, 2048], replicated
- grad_norm_gain: float32 [256], replicated
- grad_conv_kernel: float32 [49, 256], replicated
- grad_patch_weight: float32 [48, 256], replicated
- grad_patch_bias: float32 [256], replicated
Inputs may be any that keep to these rules, and one draw needn't show every extreme that they name: `latents`: each latent row has its own scale.
All inputs are finite; a program needn't handle non-finite values.
Results may differ from a plain program's by a relative error of at most 0.035.
The roundings to bfloat16 on the way count: a program that leaves them out, or rounds other values in their place, can miss the bound.
Values may be sent and summed in bfloat16 or wider, within the bound.
No kernel may reach another device: no remote copies, remote signals or barrier semaphores. Data moves between devices by JAX's collectives and lax.ppermute only.
A program may use at most 576 MiB of HBM per device.

v0:
```python
import jax
import jax.numpy as jnp
from jax import lax
from jax.sharding import PartitionSpec as P

PATCH = 4
KSIZE = 7
HEADS = 8
norm_eps = 1e-05


def padded_2(x, sides, width):
    for axis, dim in sides:
        devices, length = (lax.axis_size(axis), x.shape[dim])
        up = [(i, (i + 1) % devices) for i in range(devices - 1)]
        down = [(j, i) for i, j in up]
        last = lax.slice_in_dim(x, length - width, length, axis=dim)
        leading = lax.slice_in_dim(x, 0, width, axis=dim)
        before = lax.ppermute(last, axis, up)
        after = lax.ppermute(leading, axis, down)
        x = jnp.concatenate([before, x, after], axis=dim)
    return x


def patch_rows(pixels):
    in_channels, height, image_width = pixels.shape
    blocks = pixels.reshape(in_channels, height // PATCH, PATCH, image_width // PATCH, PATCH)
    blocks = blocks.transpose(1, 3, 0, 2, 4)
    return blocks.reshape(height // PATCH * (image_width // PATCH), in_channels * PATCH * PATCH)


def depthwise(padded, kernel, tile_rows, tile_cols):
    result = jnp.zeros((tile_rows, tile_cols, kernel.shape[1]), jnp.float32)
    for offset_row in range(KSIZE):
        for offset_col in range(KSIZE):
            window = padded[
                offset_row : offset_row + tile_rows, offset_col : offset_col + tile_cols
            ].astype(jnp.float32)
            result = result + window * kernel[offset_row * KSIZE + offset_col]
    return result


def transposed(padded, kernel, tile_rows, tile_cols):
    result = jnp.zeros((tile_rows, tile_cols, kernel.shape[1]), jnp.float32)
    last = KSIZE - 1
    for offset_row in range(KSIZE):
        for offset_col in range(KSIZE):
            start_row = last - offset_row
            start_col = last - offset_col
            window = padded[
                start_row : start_row + tile_rows, start_col : start_col + tile_cols
            ].astype(jnp.float32)
            result = result + window * kernel[offset_row * KSIZE + offset_col]
    return result


def kernel_grad(padded, upstream, tile_rows, tile_cols):
    upstream_f = upstream.astype(jnp.float32)
    kernel_terms = []
    for offset_row in range(KSIZE):
        for offset_col in range(KSIZE):
            window = padded[
                offset_row : offset_row + tile_rows, offset_col : offset_col + tile_cols
            ].astype(jnp.float32)
            kernel_terms.append(jnp.sum(window * upstream_f, axis=(0, 1)))
    return jnp.stack(kernel_terms)


def normalize(mixed):
    centre = mixed - jnp.mean(mixed, axis=-1, keepdims=True)
    variance = jnp.mean(centre * centre, axis=-1, keepdims=True)
    inverse = lax.rsqrt(variance + norm_eps)
    return (centre * inverse, inverse)


def split_heads(matrix, head_count):
    return matrix.reshape(matrix.shape[0], head_count, -1).transpose(1, 0, 2)


def merge_heads(stacked):
    return stacked.transpose(1, 0, 2).reshape(stacked.shape[1], -1)


def head_state(pieces):
    queries, key_rows, values = pieces
    score_scale = queries.shape[-1] ** (-0.5)
    scores = (
        jnp.einsum("le,te->lt", queries, key_rows, preferred_element_type=jnp.float32) * score_scale
    )
    top_score = jnp.max(scores, axis=1)
    raised = jnp.exp(scores - top_score[:, None])
    weighted = jnp.dot(raised.astype(jnp.bfloat16), values, preferred_element_type=jnp.float32)
    return (top_score, jnp.sum(raised, axis=1), weighted)


def head_grads(pieces):
    queries, key_rows, values, top_score, sum_exp, row_dots, upstream = pieces
    score_scale = queries.shape[-1] ** (-0.5)
    scores = (
        jnp.einsum("le,te->lt", queries, key_rows, preferred_element_type=jnp.float32) * score_scale
    )
    probs = jnp.exp(scores - top_score[:, None]) / sum_exp[:, None]
    d_probs = jnp.einsum("le,te->lt", upstream, values, preferred_element_type=jnp.float32)
    d_scores = (probs * (d_probs - row_dots[:, None]) * score_scale).astype(jnp.bfloat16)
    q_grad = jnp.einsum("lt,te->le", d_scores, key_rows, preferred_element_type=jnp.float32)
    k_grad = jnp.einsum("lt,le->te", d_scores, queries, preferred_element_type=jnp.float32).astype(
        jnp.bfloat16
    )
    v_grad = jnp.einsum(
        "lt,le->te", probs.astype(jnp.bfloat16), upstream, preferred_element_type=jnp.float32
    )
    return (q_grad, k_grad, v_grad.astype(jnp.bfloat16))


def rescaled(local_top, local_sum, local_weighted, top_score):
    factor = jnp.exp(local_top - top_score)
    latent_count, head_count = factor.shape
    weighted = local_weighted.reshape(latent_count, head_count, -1) * factor[:, :, None]
    return (local_sum * factor, weighted.reshape(latent_count, -1))


def normalized(weighted, sum_exp):
    latent_count, head_count = sum_exp.shape
    return (weighted.reshape(latent_count, head_count, -1) / sum_exp[:, :, None]).reshape(
        latent_count, -1
    )


def per_device(
    pixels, patch_weight, patch_bias, conv_kernel, norm_gain, kv_weight, latents, d_attended
):
    tile_rows = pixels.shape[1] // PATCH
    tile_cols = pixels.shape[2] // PATCH
    channels = patch_weight.shape[1]
    model_dim = latents.shape[1]
    latent_count = latents.shape[0]
    patches = patch_rows(pixels)
    embedded = (
        jnp.dot(patches, patch_weight, preferred_element_type=jnp.float32) + patch_bias
    ).astype(jnp.bfloat16)
    embedded = embedded.reshape(tile_rows, tile_cols, channels)
    padded = padded_2(embedded, (("rows", 0), ("cols", 1)), KSIZE // 2)
    mixed = embedded.astype(jnp.float32) + depthwise(padded, conv_kernel, tile_rows, tile_cols)
    centred, inverse = normalize(mixed)
    normed = (centred * norm_gain).astype(jnp.bfloat16).reshape(tile_rows * tile_cols, channels)
    projected = jnp.dot(normed, kv_weight, preferred_element_type=jnp.float32).astype(jnp.bfloat16)
    query_heads = split_heads(latents, HEADS)
    key_heads = split_heads(projected[:, :model_dim], HEADS)
    value_heads = split_heads(projected[:, model_dim:], HEADS)
    tops, sums, weighteds = lax.map(head_state, (query_heads, key_heads, value_heads))
    local_top = tops.T
    local_sum = sums.T
    local_weighted = merge_heads(weighteds)
    top_score = lax.pmax(local_top, ("rows", "cols"))
    part_sum, part_weighted = rescaled(local_top, local_sum, local_weighted, top_score)
    sum_exp, weighted = lax.psum((part_sum, part_weighted), ("rows", "cols"))
    attended = normalized(weighted, sum_exp)
    row_dots = jnp.sum(
        d_attended.astype(jnp.float32).reshape(latent_count, HEADS, -1)
        * attended.reshape(latent_count, HEADS, -1),
        axis=2,
    )
    q_grads, k_grads, v_grads = lax.map(
        head_grads,
        (
            query_heads,
            key_heads,
            value_heads,
            top_score.T,
            sum_exp.T,
            row_dots.T,
            split_heads(d_attended, HEADS),
        ),
    )
    local_latents = merge_heads(q_grads)
    d_projected = jnp.concatenate([merge_heads(k_grads), merge_heads(v_grads)], axis=1)
    local_kv = jnp.einsum("tc,tk->ck", normed, d_projected, preferred_element_type=jnp.float32)
    d_normed = jnp.einsum("tk,ck->tc", d_projected, kv_weight, preferred_element_type=jnp.float32)
    d_normed = d_normed.reshape(tile_rows, tile_cols, channels)
    local_gain = jnp.sum(d_normed * centred, axis=(0, 1))
    scaled = d_normed * norm_gain
    d_mixed = inverse * (
        scaled
        - jnp.mean(scaled, axis=-1, keepdims=True)
        - centred * jnp.mean(scaled * centred, axis=-1, keepdims=True)
    )
    d_mixed = d_mixed.astype(jnp.bfloat16)
    local_kernel = kernel_grad(padded, d_mixed, tile_rows, tile_cols)
    d_padded = padded_2(d_mixed, (("rows", 0), ("cols", 1)), KSIZE // 2)
    d_embedded = (
        d_mixed.astype(jnp.float32) + transposed(d_padded, conv_kernel, tile_rows, tile_cols)
    ).astype(jnp.bfloat16)
    d_embedded = d_embedded.reshape(tile_rows * tile_cols, channels)
    local_patch = jnp.einsum("tp,tc->pc", patches, d_embedded, preferred_element_type=jnp.float32)
    local_bias = jnp.sum(d_embedded.astype(jnp.float32), axis=0)
    grad_latents, grad_kv, grad_gain, grad_kernel, grad_patch, grad_bias = lax.psum(
        (local_latents, local_kv, local_gain, local_kernel, local_patch, local_bias),
        ("rows", "cols"),
    )
    return (attended, grad_latents, grad_kv, grad_gain, grad_kernel, grad_patch, grad_bias)


def solution(mesh):
    return jax.shard_map(
        per_device,
        mesh=mesh,
        in_specs=(P(None, "rows", "cols"), P(), P(), P(), P(), P(), P(), P()),
        out_specs=(P(), P(), P(), P(), P(), P(), P()),
        check_vma=False,
    )
```

profile of v0, /device:TPU:1, one launch (start us, length us, event | category | flops | bytes accessed | tf_op | source)
XLA Modules:
  0.0 872.1 jit_solution(149863310632694244)
XLA Ops:
  7.2 15.3 %reshape.154 = bf16[3,32,4,64,4]{4,3,2,1,0:T(8,128)(2,1)} reshape(bf16[3,128,256]{2,1,0:T(8,128)(2,1)} %param.12) | data formatting | bytes 393216 | tf_op jit(solution)/shard_map/reshape | solution.py:27
  22.6 6.0 copy.22
  29.5 3.3 collective-permute-start.1
  32.8 3.5 collective-permute-start
  38.1 3.2 collective-permute-start.2
  48.9 19.2 %fusion.180 = (f32[32,64]{1,0:T(8,128)S(1)}, f32[32,64,256]{2,1,0:T(8,128)S(1)}) fusion(f32[256]{0:T(256)} %bitcast.382, bf16[38,67,256]{2,1,0:T(8,128)(2,1)S(1)} %get-tuple-element.249, f32[256]{0:T(256)} %bitcast.384, f32[256]{0:T(256)S(1)} %bitcast.290, f32[256]{0:T(256)S(1)} %bitcast.292, bf16[3,64,256]{2,1,0:T(8,128)(2,1)S(1)} %copy-done.16, ...), kind=kLoop, calls=%fused_computation.344 | loop fusion | flops 80738304 | bytes 47440896 | tf_op jit(solution)/shard_map/reduce_sum | solution.py:70
  69.6 2.4 convolution_convert_fusion.2
  72.0 3.6 fusion.182
  75.6 6.4 copy.24
  82.0 6.4 copy.23
  88.6 39.8 %while.28 = (s32[]{:T(128)}, f32[8,256]{1,0:T(8,128)S(1)}, f32[8,256]{1,0:T(8,128)}, f32[8,256,128]{2,1,0:T(8,128)S(1)}, bf16[8,256,128]{2,1,0:T(8,128)(2,1)}, /...) while((s32[]{:T(128)}, f32[8,256]{1,0:T(8,128)S(1)}, ...), condition=%wide.region_5.6_spmd, body=%wide.region_2.5_spmd.sunk | while | flops 271580672 | bytes 7546989 | solution.py:150
  128.9 69.0 %pmax.7 = f32[256,8]{0,1:T(8,128)S(1)} all-reduce(f32[256,8]{0,1:T(8,128)} %bitcast.284), channel_id=1, replica_groups=mesh['rows'=8,'cols'=16] {'rows','cols'}, use_global_device_ids=true, to_apply=%region_6.7 | all-reduce | flops 2048 | bytes 16384 | tf_op jit(solution)/shard_map/pmax | solution.py:154
  202.7 64.4 %psum.57 = f32[256,8]{0,1:T(8,128)S(1)} all-reduce(f32[256,8]{0,1:T(8,128)S(1)} %copy-done.32), channel_id=1, replica_groups=mesh['rows'=8,'cols'=16] {'rows','cols'}, use_global_device_ids=true, to_apply=%region_8.9 | all-reduce | flops 2048 | bytes 16384 | tf_op jit(solution)/shard_map/psum | solution.py:156
  267.1 78.4 %all-reduce.6.cloned.1.call-done = f32[256,1024]{1,0:T(8,128)} async-done(((f32[256,1024]{1,0:T(8,128)}), f32[256,1024]{1,0:T(8,128)}) %all-reduce.6.cloned.1.call-update) | async-done | bytes 1048592 | tf_op jit(solution)/shard_map/psum | solution.py:156
  350.0 126.1 %while.29 = (s32[]{:T(128)}, f32[8,256,128]{2,1,0:T(8,128)}, bf16[8,2048,128]{1,2,0:T(8,128)(2,1)}, bf16[8,2048,128]{1,2,0:T(8,128)(2,1)}, bf16[8,256,128]{2,1,0...) while((s32[]{:T(128)}, f32[8,256,128]{2,1,0:T(8,128)}, ...), condition=%wide.region_11.12_spmd, body=%wide.region_10.11_spmd.sunk | while | flops 675807232 | bytes 16658581 | solution.py:163
  352.3 2.1 fusion.238
  356.1 2.1 copy.46
  358.1 2.1 fusion.239
  360.3 2.1 fusion.237
  363.6 2.1 constant_dynamic-update-slice_fusion.3
  368.1 2.1 fusion.238
  371.9 2.1 copy.46
  373.9 2.1 fusion.239
  376.1 2.1 fusion.237
  379.4 2.2 constant_dynamic-update-slice_fusion.3
  384.0 2.1 fusion.238
  387.7 2.1 copy.46
  389.7 2.1 fusion.239
  391.9 2.1 fusion.237
  395.3 2.1 constant_dynamic-update-slice_fusion.3
  399.7 2.1 fusion.238
  405.5 2.1 fusion.239
  407.6 2.1 fusion.237
  411.0 2.1 constant_dynamic-update-slice_fusion.3
  415.4 2.1 fusion.238
  421.2 2.1 fusion.239
  423.4 2.1 fusion.237
  426.7 2.1 constant_dynamic-update-slice_fusion.3
  431.2 2.1 fusion.238
  437.0 2.1 fusion.239
  439.1 2.1 fusion.237
  442.5 2.1 constant_dynamic-update-slice_fusion.3
  447.0 2.1 fusion.238
  452.8 2.1 fusion.239
  454.9 2.1 fusion.237
  458.3 2.1 constant_dynamic-update-slice_fusion.3
  462.7 2.1 fusion.238
  468.5 2.1 fusion.239
  470.6 2.1 fusion.237
  474.0 2.1 constant_dynamic-update-slice_fusion.3
  476.1 7.3 multiply_reduce_fusion.1
  484.1 4.5 multiply_reduce_fusion
  488.6 6.6 fusion.137
  495.3 6.5 fusion.141
  501.7 2.9 collective-permute-start.4
  504.7 2.4 collective-permute-start.5
  507.1 5.6 fusion.140
  512.8 8.2 fusion.43
  523.1 4.6 collective-permute-start.7
  529.4 9.1 %stack.199 = f32[49,256]{1,0:T(8,128)} concatenate(f32[1,256]{1,0:T(1,128)} %bitcast.434, f32[1,256]{1,0:T(1,128)} %bitcast.433, f32[1,256]{1,0:T(1,128)} %bitcast.432, f32[1,256]{1,0:T(1,128)} %bitcast.428, f32[1,256]{1,0:T(1,128)} %bitcast.424, f32[1,256]{1,0:T(1,128)} %bitcast.423, f32[1,256]{1,0:T(1,128)} %bitcast.405, f32[1,256]{1,0:T(1,128)S(1)} %bitcast.387, ...), dimensions={0} | concatenate | bytes 100352 | tf_op jit(solution)/shard_map/stack | solution.py:66
  541.0 21.4 %convert_reduce_fusion = (f32[256]{0:T(256)}, bf16[32,64,256]{2,1,0:T(8,128)(2,1)S(1)}) fusion(f32[256]{0:T(256)} %bitcast.383, bf16[38,67,256]{2,1,0:T(8,128)(2,1)S(1)} %get-tuple-element.245, f32[256]{0:T(256)} %bitcast.385, f32[256]{0:T(256)S(1)} %bitcast.291, f32[256]{0:T(256)S(1)} %bitcast.293, bf16[32,64,256]{2,1,0:T(8,128)(2,1)S(1)} %get-tuple-element.233, ...), kind=kLoop, calls=%fused_computation.283 | loop fusion | flops 81788672 | bytes 46385152 | tf_op jit(solution)/shard_map/reduce_sum | solution.py:195
  568.5 135.2 %all-reduce.8.cloned.1.call-done = (f32[256]{0:T(256)}, f32[49,256]{1,0:T(8,128)}, f32[48,256]{1,0:T(8,128)}, f32[256]{0:T(256)}) async-done(((f32[256]{0:T(256)}, f32[49,256]{1,0:T(8,128)}, f32[48,256]{1,0:T(8,128)}, f32[256]{0:T(256)}), (f32[256]{0:T(256)}, f32[49,256]{1,0:T(8,128)}, f32[48,256]{1,0:T(8,128)}, f32[256]{0:T(256)})) %all-reduce.8.cloned.1.call-update) | async-done | bytes 101392 | tf_op jit(solution)/shard_map/psum | solution.py:196
  703.7 155.7 %all-reduce.10.cloned.1.call-done = (f32[256,1024]{1,0:T(8,128)}, f32[256,2048]{1,0:T(8,128)}) async-done(((f32[256,1024]{1,0:T(8,128)}, f32[256,2048]{1,0:T(8,128)}), (f32[256,1024]{1,0:T(8,128)}, f32[256,2048]{1,0:T(8,128)})) %all-reduce.10.cloned.1.call-update) | async-done | bytes 3145744 | tf_op jit(solution)/shard_map/psum | solution.py:196
  859.4 2.5 copy.87
  (399 shorter events, 128.1 us)
Async XLA Ops:
  7.2 62.4 %copy-start = (bf16[256,2048]{1,0:T(8,128)(2,1)S(1)}, bf16[256,2048]{1,0:T(8,128)(2,1)}, u32[]{:S(2)}) copy-start(bf16[256,2048]{1,0:T(8,128)(2,1)} %param.17) | copy-start | bytes 3145732
  7.2 338.3 %all-reduce.6.cloned.1.call-start = ((), (), s32[]{:S(2)}) async-start(), calls=%async_computation | async-start | bytes 2097152 | tf_op jit(solution)/shard_map/psum | solution.py:156
  22.6 6.4 copy-start.33
  22.6 6.4 copy-start.121
  28.6 7.8 copy-start.30
  28.6 14.8 %copy-start.25 = (bf16[256,1024]{1,0:T(8,128)(2,1)S(1)}, bf16[256,1024]{1,0:T(8,128)(2,1)}, u32[]{:S(2)}) copy-start(bf16[256,1024]{1,0:T(8,128)(2,1)} %param.18) | copy-start | bytes 1572868
  29.0 14.4 %copy-start.13 = (bf16[2048,48]{0,1:T(8,128)(2,1)}, bf16[2048,48]{0,1:T(8,128)(2,1)S(1)}, u32[]{:S(2)}) copy-start(bf16[2048,48]{0,1:T(8,128)(2,1)S(1)} %reshape.155) | copy-start | bytes 589828
  29.5 19.1 %copy-start.5 = (bf16[2048,256]{1,0:T(8,128)(2,1)}, bf16[2048,256]{1,0:T(8,128)(2,1)S(1)}, u32[]{:S(2)}) copy-start(bf16[2048,256]{1,0:T(8,128)(2,1)S(1)} %fusion.44) | copy-start | bytes 3145732
  29.5 8.2 collective-permute-start.1
  32.8 5.2 collective-permute-start
  37.7 5.7 copy-start.15
  38.0 5.4 copy-start.18
  38.1 6.9 collective-permute-start.2
  41.3 5.6 collective-permute-start.3
  44.7 3.9 copy-start.37
  44.7 3.9 copy-start.39
  44.7 3.9 copy-start.41
  44.7 3.9 copy-start.43
  44.7 3.9 copy-start.45
  44.7 3.9 copy-start.47
  44.7 3.9 copy-start.49
  44.7 3.9 copy-start.51
  44.7 3.9 copy-start.53
  44.7 3.9 copy-start.55
  44.8 3.9 copy-start.57
  44.8 3.9 copy-start.59
  44.8 3.9 copy-start.61
  44.8 3.9 copy-start.63
  44.8 3.9 copy-start.65
  44.8 3.9 copy-start.67
  44.8 3.9 copy-start.69
  44.8 3.9 copy-start.71
  44.8 3.9 copy-start.73
  44.8 3.9 copy-start.75
  48.5 19.6 %copy-start.1 = (bf16[38,67,256]{2,1,0:T(8,128)(2,1)}, bf16[38,67,256]{2,1,0:T(8,128)(2,1)S(1)}, u32[]{:S(2)}) copy-start(bf16[38,67,256]{2,1,0:T(8,128)(2,1)S(1)} %get-tuple-element.249) | copy-start | bytes 3910660
  200.6 503.2 %all-reduce.8.cloned.1.call-start = ((), (), s32[]{:S(2)}) async-start(), calls=%async_computation.1 | async-start | bytes 217088 | tf_op jit(solution)/shard_map/psum | solution.py:196
  476.1 8.0 copy-start.109
  484.1 4.5 copy-start.4
  484.1 4.5 copy-start.7
  484.1 4.5 copy-start.27
  488.6 6.6 copy-start.2
  495.2 11.9 %copy-start.6 = (bf16[2048,256]{1,0:T(8,128)(2,1)S(1)}, bf16[2048,256]{1,0:T(8,128)(2,1)}, u32[]{:S(2)}) copy-start(bf16[2048,256]{1,0:T(8,128)(2,1)} %copy-done.5) | copy-start | bytes 3145732
  495.2 11.9 %copy-start.17 = (bf16[3,64,256]{2,1,0:T(8,128)(2,1)S(1)}, bf16[3,64,256]{2,1,0:T(8,128)(2,1)}, u32[]{:S(2)}) copy-start(bf16[3,64,256]{2,1,0:T(8,128)(2,1)} %copy-done.15) | copy-start | bytes 294916
  495.2 11.9 %copy-start.20 = (bf16[3,64,256]{2,1,0:T(8,128)(2,1)S(1)}, bf16[3,64,256]{2,1,0:T(8,128)(2,1)}, u32[]{:S(2)}) copy-start(bf16[3,64,256]{2,1,0:T(8,128)(2,1)} %copy-done.18) | copy-start | bytes 294916
  495.2 17.5 %copy-start.123 = (bf16[8,2048,128]{1,2,0:T(8,128)(2,1)S(1)}, bf16[8,2048,128]{1,2,0:T(8,128)(2,1)}, u32[]{:S(2)}) copy-start(bf16[8,2048,128]{1,2,0:T(8,128)(2,1)} %get-tuple-element.109) | copy-start | bytes 12582916
  501.7 19.3 %collective-permute-start.4 = (bf16[3,64,256]{2,1,0:T(8,128)(2,1)S(1)}, bf16[3,64,256]{2,1,0:T(8,128)(2,1)S(1)}, u32[]{:S(2)}, u32[]{:S(2)}) collective-permute-start(bf16[3,64,256]{2,1,0:T(8,128)(2,1)S(1)} %get-tuple-element.252), channel_id=1, source_target_pairs={{0,16},{16,32},{32,48},{48,64},{64,80},{80,96},{96,112},{1,17},{17... | collective-permute-start | bytes 294920 | tf_op jit(solution)/shard_map/ppermute | solution.py:19
  504.6 8.1 copy-start.9
  504.6 8.1 copy-start.122
  504.7 16.4 %collective-permute-start.5 = (bf16[3,64,256]{2,1,0:T(8,128)(2,1)S(1)}, bf16[3,64,256]{2,1,0:T(8,128)(2,1)S(1)}, u32[]{:S(2)}, u32[]{:S(2)}) collective-permute-start(bf16[3,64,256]{2,1,0:T(8,128)(2,1)S(1)} %get-tuple-element.253), channel_id=1, source_target_pairs={{16,0},{32,16},{48,32},{64,48},{80,64},{96,80},{112,96},{17,1},{33... | collective-permute-start | bytes 294920 | tf_op jit(solution)/shard_map/ppermute | solution.py:20
  521.0 8.3 copy-start.21
  521.0 8.3 copy-start.23
  521.8 17.1 %collective-permute-start.6 = (bf16[38,3,256]{2,1,0:T(4,128)(2,1)}, bf16[38,3,256]{2,1,0:T(4,128)(2,1)}, u32[]{:S(2)}, u32[]{:S(2)}) collective-permute-start(bf16[38,3,256]{2,1,0:T(4,128)(2,1)} %get-tuple-element.246), channel_id=1, source_target_pairs={{1,0},{2,1},{3,2},{4,3},{5,4},{6,5},{7,6},{8,7},{9,8},{10,9},{11,1... | collective-permute-start | bytes 175112 | tf_op jit(solution)/shard_map/ppermute | solution.py:20
  523.0 6.2 copy-start.110
  523.1 6.2 copy-start.111
  523.1 6.2 copy-start.112
  523.1 6.2 copy-start.113
  523.1 6.2 copy-start.114
  523.1 6.2 copy-start.115
  523.1 6.2 copy-start.116
  523.1 6.2 copy-start.117
  523.1 6.2 copy-start.118
  523.1 15.7 %collective-permute-start.7 = (bf16[38,3,256]{2,1,0:T(4,128)(2,1)}, bf16[38,3,256]{2,1,0:T(4,128)(2,1)}, u32[]{:S(2)}, u32[]{:S(2)}) collective-permute-start(bf16[38,3,256]{2,1,0:T(4,128)(2,1)} %get-tuple-element.247), channel_id=1, source_target_pairs={{0,1},{1,2},{2,3},{3,4},{4,5},{5,6},{6,7},{7,8},{8,9},{9,10},{10,1... | collective-permute-start | bytes 175112 | tf_op jit(solution)/shard_map/ppermute | solution.py:19
  541.0 21.4 %copy-start.14 = (bf16[2048,48]{0,1:T(8,128)(2,1)S(1)}, bf16[2048,48]{0,1:T(8,128)(2,1)}, u32[]{:S(2)}) copy-start(bf16[2048,48]{0,1:T(8,128)(2,1)} %copy-done.13) | copy-start | bytes 589828
  563.3 296.1 %all-reduce.10.cloned.1.call-start = ((), (), s32[]{:S(2)}) async-start(), calls=%async_computation.2 | async-start | bytes 6291456 | tf_op jit(solution)/shard_map/psum | solution.py:196
  (71 other events, 180.0 us)
Sparse Core Ops, SparseCore 0:
  200.7 144.7 all-reduce.5
  563.4 140.2 all-reduce.7
  709.1 150.2 all-reduce.9
where the time goes:
time: 877 us; the launch traced here: 872 us
  waiting for transfers between devices  371 us (42%)
  blocking collectives  133 us (15%)
  local copies, waits for them, and re-layouts  128 us (15%)
  matrix products  122 us (14%)
  other arithmetic  79.9 us (9%)
  starting transfers between devices  22.9 us (3%)
  between operations  15.6 us (2%)
    psum x2, waiting for transfers between devices, per_device(): lax.psum((local_latents, local_kv, local_gain, local_kernel, local_patch,...  291 us
    psum x1, waiting for transfers between devices, per_device(): sum_exp, weighted = lax.psum((part_sum, part_weighted), ('rows', 'cols'))  78.4 us
    pmax x1, blocking collectives, per_device(): top_score = lax.pmax(local_top, ('rows', 'cols'))  69 us
    psum x1, blocking collectives, per_device(): sum_exp, weighted = lax.psum((part_sum, part_weighted), ('rows', 'cols'))  64.4 us
    dynamic_update_slice x24, local copies, waits for them, and re-layouts, per_device(): lax.map(head_grads, (query_heads, key_heads, value_heads, top_score.T, su...  43.4 us
    reduce_sum x1, other arithmetic, per_device(): local_bias = jnp.sum(d_embedded.astype(jnp.float32), axis=0)  21.4 us
    reduce_sum x4, other arithmetic, kernel_grad(): kernel_terms.append(jnp.sum(window * upstream_f, axis=(0, 1)))  20.2 us
    reduce_sum x1, other arithmetic, normalize(): centre = mixed - jnp.mean(mixed, axis=-1, keepdims=True)  19.2 us
  transfers between devices with their start and end apart: 11, of which 5 were waited for; matrix products, arithmetic and copies ran while one was open for 4% of the time, Pallas kernels for 0%

commit v1 on v0

--- a/solution.py
+++ b/solution.py
@@ -194,8 +194,10 @@
     local_patch = jnp.einsum("tp,tc->pc", patches, d_embedded, preferred_element_type=jnp.float32)
     local_bias = jnp.sum(d_embedded.astype(jnp.float32), axis=0)
     grad_latents, grad_kv, grad_gain, grad_kernel, grad_patch, grad_bias = lax.psum(
-        (local_latents, local_kv, local_gain, local_kernel, local_patch, local_bias),
-        ("rows", "cols"),
+        lax.psum(
+            (local_latents, local_kv, local_gain, local_kernel, local_patch, local_bias), "cols"
+        ),
+        "rows",
     )
     return (attended, grad_latents, grad_kv, grad_gain, grad_kernel, grad_patch, grad_bias)
 

time: 877 us -> 893 us (1.018)
  waiting for transfers between devices: 371 us -> 385 us
    psum x0 -> x2, waiting for transfers between devices: none -> 126 us  [per_device(): lax.psum(lax.psum((local_latents, local_kv, local_gain, local_kernel, loc...]
    psum x2, waiting for transfers between devices: 291 us -> 180 us  [per_device(): lax.psum((local_latents, local_kv, local_gain, local_kernel, local_patch,...]
  transfers between devices with their start and end apart: 11 -> 13, of which waited for: 5 -> 7; matrix products, arithmetic and copies ran while one was open for 4% -> 4% of each run, Pallas kernels for 0% -> 0%
where the time goes in v1:
time: 893 us; the launch traced here: 887 us
  waiting for transfers between devices  385 us (43%)
  blocking collectives  133 us (15%)
  local copies, waits for them, and re-layouts  128 us (14%)
  matrix products  122 us (14%)
  other arithmetic  79.9 us (9%)
  starting transfers between devices  23 us (3%)
  between operations  15.6 us (2%)
    psum x2, waiting for transfers between devices, per_device(): lax.psum((local_latents, local_kv, local_gain, local_kernel, local_patch,...  180 us
    psum x2, waiting for transfers between devices, per_device(): lax.psum(lax.psum((local_latents, local_kv, local_gain, local_kernel, loc...  126 us
    psum x1, waiting for transfers between devices, per_device(): sum_exp, weighted = lax.psum((part_sum, part_weighted), ('rows', 'cols'))  78.4 us
    pmax x1, blocking collectives, per_device(): top_score = lax.pmax(local_top, ('rows', 'cols'))  69 us
    psum x1, blocking collectives, per_device(): sum_exp, weighted = lax.psum((part_sum, part_weighted), ('rows', 'cols'))  64.4 us
    dynamic_update_slice x24, local copies, waits for them, and re-layouts, per_device(): lax.map(head_grads, (query_heads, key_heads, value_heads, top_score.T, su...  43.4 us
    reduce_sum x1, other arithmetic, per_device(): local_bias = jnp.sum(d_embedded.astype(jnp.float32), axis=0)  21.4 us
    reduce_sum x4, other arithmetic, kernel_grad(): kernel_terms.append(jnp.sum(window * upstream_f, axis=(0, 1)))  20.2 us
  transfers between devices with their start and end apart: 13, of which 7 were waited for; matrix products, arithmetic and copies ran while one was open for 4% of the time, Pallas kernels for 0%

profile of v1, /device:TPU:1, one launch (start us, length us, event | category | flops | bytes accessed | tf_op | source)
XLA Modules:
  0.0 886.7 jit_solution(7710292637918321966)
XLA Ops:
  7.2 15.3 %reshape.154 = bf16[3,32,4,64,4]{4,3,2,1,0:T(8,128)(2,1)} reshape(bf16[3,128,256]{2,1,0:T(8,128)(2,1)} %param.12) | data formatting | bytes 393216 | tf_op jit(solution)/shard_map/reshape | solution.py:27
  22.6 6.0 copy.22
  29.5 3.3 collective-permute-start.1
  32.8 3.5 collective-permute-start
  38.1 3.2 collective-permute-start.2
  48.9 19.2 %fusion.180 = (f32[32,64]{1,0:T(8,128)S(1)}, f32[32,64,256]{2,1,0:T(8,128)S(1)}) fusion(f32[256]{0:T(256)} %bitcast.382, bf16[38,67,256]{2,1,0:T(8,128)(2,1)S(1)} %get-tuple-element.255, f32[256]{0:T(256)} %bitcast.384, f32[256]{0:T(256)S(1)} %bitcast.290, f32[256]{0:T(256)S(1)} %bitcast.292, bf16[3,64,256]{2,1,0:T(8,128)(2,1)S(1)} %copy-done.16, ...), kind=kLoop, calls=%fused_computation.344 | loop fusion | flops 80738304 | bytes 47440896 | tf_op jit(solution)/shard_map/reduce_sum | solution.py:70
  69.6 2.4 convolution_convert_fusion.2
  72.0 3.6 fusion.182
  75.6 6.4 copy.24
  82.0 6.4 copy.23
  88.6 39.8 %while.28 = (s32[]{:T(128)}, f32[8,256]{1,0:T(8,128)S(1)}, f32[8,256]{1,0:T(8,128)}, f32[8,256,128]{2,1,0:T(8,128)S(1)}, bf16[8,256,128]{2,1,0:T(8,128)(2,1)}, /...) while((s32[]{:T(128)}, f32[8,256]{1,0:T(8,128)S(1)}, ...), condition=%wide.region_5.6_spmd, body=%wide.region_2.5_spmd.sunk | while | flops 271580672 | bytes 7546989 | solution.py:150
  128.9 69.0 %pmax.7 = f32[256,8]{0,1:T(8,128)S(1)} all-reduce(f32[256,8]{0,1:T(8,128)} %bitcast.284), channel_id=1, replica_groups=mesh['rows'=8,'cols'=16] {'rows','cols'}, use_global_device_ids=true, to_apply=%region_6.7 | all-reduce | flops 2048 | bytes 16384 | tf_op jit(solution)/shard_map/pmax | solution.py:154
  202.7 64.4 %psum.99 = f32[256,8]{0,1:T(8,128)S(1)} all-reduce(f32[256,8]{0,1:T(8,128)S(1)} %copy-done.32), channel_id=1, replica_groups=mesh['rows'=8,'cols'=16] {'rows','cols'}, use_global_device_ids=true, to_apply=%region_8.9 | all-reduce | flops 2048 | bytes 16384 | tf_op jit(solution)/shard_map/psum | solution.py:156
  267.1 78.4 %all-reduce.10.cloned.1.call-done = f32[256,1024]{1,0:T(8,128)} async-done(((f32[256,1024]{1,0:T(8,128)}), f32[256,1024]{1,0:T(8,128)}) %all-reduce.10.cloned.1.call-update) | async-done | bytes 1048592 | tf_op jit(solution)/shard_map/psum | solution.py:156
  350.0 126.1 %while.29 = (s32[]{:T(128)}, f32[8,256,128]{2,1,0:T(8,128)}, bf16[8,2048,128]{1,2,0:T(8,128)(2,1)}, bf16[8,2048,128]{1,2,0:T(8,128)(2,1)}, bf16[8,256,128]{2,1,0...) while((s32[]{:T(128)}, f32[8,256,128]{2,1,0:T(8,128)}, ...), condition=%wide.region_11.12_spmd, body=%wide.region_10.11_spmd.sunk | while | flops 675807232 | bytes 16658581 | solution.py:163
  352.3 2.1 fusion.238
  356.1 2.1 copy.46
  358.1 2.1 fusion.239
  360.3 2.1 fusion.237
  363.6 2.1 constant_dynamic-update-slice_fusion.3
  368.1 2.1 fusion.238
  373.9 2.1 fusion.239
  376.1 2.1 fusion.237
  379.4 2.2 constant_dynamic-update-slice_fusion.3
  384.0 2.1 fusion.238
  389.7 2.1 fusion.239
  391.9 2.1 fusion.237
  395.3 2.1 constant_dynamic-update-slice_fusion.3
  399.7 2.1 fusion.238
  405.5 2.1 fusion.239
  407.6 2.1 fusion.237
  411.0 2.1 constant_dynamic-update-slice_fusion.3
  415.4 2.1 fusion.238
  421.2 2.1 fusion.239
  423.4 2.1 fusion.237
  426.7 2.1 constant_dynamic-update-slice_fusion.3
  431.2 2.1 fusion.238
  437.0 2.1 fusion.239
  439.1 2.1 fusion.237
  442.5 2.1 constant_dynamic-update-slice_fusion.3
  447.0 2.1 fusion.238
  452.8 2.1 fusion.239
  454.9 2.1 fusion.237
  458.3 2.1 constant_dynamic-update-slice_fusion.3
  462.7 2.1 fusion.238
  468.5 2.1 fusion.239
  470.6 2.1 fusion.237
  474.0 2.1 constant_dynamic-update-slice_fusion.3
  476.1 7.3 multiply_reduce_fusion.1
  484.1 4.5 multiply_reduce_fusion
  488.6 6.6 fusion.137
  495.2 6.5 fusion.141
  501.7 2.9 collective-permute-start.4
  504.6 2.4 collective-permute-start.5
  507.1 5.6 fusion.140
  512.7 8.2 fusion.43
  523.1 4.6 collective-permute-start.7
  529.3 9.1 %stack.199 = f32[49,256]{1,0:T(8,128)} concatenate(f32[1,256]{1,0:T(1,128)} %bitcast.434, f32[1,256]{1,0:T(1,128)} %bitcast.433, f32[1,256]{1,0:T(1,128)} %bitcast.432, f32[1,256]{1,0:T(1,128)} %bitcast.428, f32[1,256]{1,0:T(1,128)} %bitcast.424, f32[1,256]{1,0:T(1,128)} %bitcast.423, f32[1,256]{1,0:T(1,128)} %bitcast.405, f32[1,256]{1,0:T(1,128)S(1)} %bitcast.387, ...), dimensions={0} | concatenate | bytes 100352 | tf_op jit(solution)/shard_map/stack | solution.py:66
  540.9 21.4 %convert_reduce_fusion = (f32[256]{0:T(256)}, bf16[32,64,256]{2,1,0:T(8,128)(2,1)S(1)}) fusion(f32[256]{0:T(256)} %bitcast.383, bf16[38,67,256]{2,1,0:T(8,128)(2,1)S(1)} %get-tuple-element.251, f32[256]{0:T(256)} %bitcast.385, f32[256]{0:T(256)S(1)} %bitcast.291, f32[256]{0:T(256)S(1)} %bitcast.293, bf16[32,64,256]{2,1,0:T(8,128)(2,1)S(1)} %get-tuple-element.239, ...), kind=kLoop, calls=%fused_computation.283 | loop fusion | flops 81788672 | bytes 46385152 | tf_op jit(solution)/shard_map/reduce_sum | solution.py:195
  564.8 79.6 %all-reduce.12.cloned.1.call-done = (f32[256]{0:T(256)}, f32[49,256]{1,0:T(8,128)}, f32[48,256]{1,0:T(8,128)}, f32[256]{0:T(256)}) async-done(((f32[256]{0:T(256)}, f32[49,256]{1,0:T(8,128)}, f32[48,256]{1,0:T(8,128)}, f32[256]{0:T(256)}), (f32[256]{0:T(256)}, f32[49,256]{1,0:T(8,128)}, f32[48,256]{1,0:T(8,128)}, f32[256]{0:T(256)})) %all-reduce.12.cloned.1.call-update) | async-done | bytes 101392 | tf_op jit(solution)/shard_map/psum | solution.py:197
  644.4 100.0 %all-reduce.14.cloned.1.call-done = (f32[256,1024]{1,0:T(8,128)}, f32[256,2048]{1,0:T(8,128)}) async-done(((f32[256,1024]{1,0:T(8,128)}, f32[256,2048]{1,0:T(8,128)}), (f32[256,1024]{1,0:T(8,128)}, f32[256,2048]{1,0:T(8,128)})) %all-reduce.14.cloned.1.call-update) | async-done | bytes 3145744 | tf_op jit(solution)/shard_map/psum | solution.py:197
  748.2 55.6 %all-reduce.16.cloned.1.call-done = (f32[256]{0:T(256)}, f32[49,256]{1,0:T(8,128)}, f32[48,256]{1,0:T(8,128)}, f32[256]{0:T(256)}) async-done(((f32[256]{0:T(256)}, f32[49,256]{1,0:T(8,128)}, f32[48,256]{1,0:T(8,128)}, f32[256]{0:T(256)}), (f32[256]{0:T(256)}, f32[49,256]{1,0:T(8,128)}, f32[48,256]{1,0:T(8,128)}, f32[256]{0:T(256)})) %all-reduce.16.cloned.1.call-update) | async-done | bytes 101392 | tf_op jit(solution)/shard_map/psum | solution.py:196
  803.7 70.3 %all-reduce.18.cloned.1.call-done = (f32[256,1024]{1,0:T(8,128)}, f32[256,2048]{1,0:T(8,128)}) async-done(((f32[256,1024]{1,0:T(8,128)}, f32[256,2048]{1,0:T(8,128)}), (f32[256,1024]{1,0:T(8,128)}, f32[256,2048]{1,0:T(8,128)})) %all-reduce.18.cloned.1.call-update) | async-done | bytes 3145744 | tf_op jit(solution)/shard_map/psum | solution.py:196
  874.0 2.5 copy.93
  (405 shorter events, 132.3 us)
Async XLA Ops:
  7.2 62.4 %copy-start = (bf16[256,2048]{1,0:T(8,128)(2,1)S(1)}, bf16[256,2048]{1,0:T(8,128)(2,1)}, u32[]{:S(2)}) copy-start(bf16[256,2048]{1,0:T(8,128)(2,1)} %param.17) | copy-start | bytes 3145732
  7.2 338.3 %all-reduce.10.cloned.1.call-start = ((), (), s32[]{:S(2)}) async-start(), calls=%async_computation | async-start | bytes 2097152 | tf_op jit(solution)/shard_map/psum | solution.py:156
  22.6 6.4 copy-start.33
  22.6 6.4 copy-start.121
  28.6 7.8 copy-start.30
  28.6 14.8 %copy-start.25 = (bf16[256,1024]{1,0:T(8,128)(2,1)S(1)}, bf16[256,1024]{1,0:T(8,128)(2,1)}, u32[]{:S(2)}) copy-start(bf16[256,1024]{1,0:T(8,128)(2,1)} %param.18) | copy-start | bytes 1572868
  29.0 14.4 %copy-start.13 = (bf16[2048,48]{0,1:T(8,128)(2,1)}, bf16[2048,48]{0,1:T(8,128)(2,1)S(1)}, u32[]{:S(2)}) copy-start(bf16[2048,48]{0,1:T(8,128)(2,1)S(1)} %reshape.155) | copy-start | bytes 589828
  29.5 19.1 %copy-start.5 = (bf16[2048,256]{1,0:T(8,128)(2,1)}, bf16[2048,256]{1,0:T(8,128)(2,1)S(1)}, u32[]{:S(2)}) copy-start(bf16[2048,256]{1,0:T(8,128)(2,1)S(1)} %fusion.44) | copy-start | bytes 3145732
  29.5 8.2 collective-permute-start.1
  32.8 5.2 collective-permute-start
  37.7 5.7 copy-start.15
  38.0 5.4 copy-start.18
  38.1 6.9 collective-permute-start.2
  41.3 5.6 collective-permute-start.3
  44.7 3.9 copy-start.37
  44.7 3.9 copy-start.39
  44.7 3.9 copy-start.41
  44.7 3.9 copy-start.43
  44.7 3.9 copy-start.45
  44.7 3.9 copy-start.47
  44.7 3.9 copy-start.49
  44.7 3.9 copy-start.51
  44.7 3.9 copy-start.53
  44.7 3.9 copy-start.55
  44.8 3.9 copy-start.57
  44.8 3.9 copy-start.59
  44.8 3.9 copy-start.61
  44.8 3.9 copy-start.63
  44.8 3.9 copy-start.65
  44.8 3.9 copy-start.67
  44.8 3.9 copy-start.69
  44.8 3.9 copy-start.71
  48.5 19.6 %copy-start.1 = (bf16[38,67,256]{2,1,0:T(8,128)(2,1)}, bf16[38,67,256]{2,1,0:T(8,128)(2,1)S(1)}, u32[]{:S(2)}) copy-start(bf16[38,67,256]{2,1,0:T(8,128)(2,1)S(1)} %get-tuple-element.255) | copy-start | bytes 3910660
  200.6 443.8 %all-reduce.12.cloned.1.call-start = ((), (), s32[]{:S(2)}) async-start(), calls=%async_computation.1 | async-start | bytes 217088 | tf_op jit(solution)/shard_map/psum | solution.py:197
  476.1 8.0 copy-start.109
  484.1 4.5 copy-start.4
  484.1 4.5 copy-start.7
  484.1 4.5 copy-start.27
  488.6 6.6 copy-start.2
  495.2 11.9 %copy-start.6 = (bf16[2048,256]{1,0:T(8,128)(2,1)S(1)}, bf16[2048,256]{1,0:T(8,128)(2,1)}, u32[]{:S(2)}) copy-start(bf16[2048,256]{1,0:T(8,128)(2,1)} %copy-done.5) | copy-start | bytes 3145732
  495.2 11.9 %copy-start.17 = (bf16[3,64,256]{2,1,0:T(8,128)(2,1)S(1)}, bf16[3,64,256]{2,1,0:T(8,128)(2,1)}, u32[]{:S(2)}) copy-start(bf16[3,64,256]{2,1,0:T(8,128)(2,1)} %copy-done.15) | copy-start | bytes 294916
  495.2 11.9 %copy-start.20 = (bf16[3,64,256]{2,1,0:T(8,128)(2,1)S(1)}, bf16[3,64,256]{2,1,0:T(8,128)(2,1)}, u32[]{:S(2)}) copy-start(bf16[3,64,256]{2,1,0:T(8,128)(2,1)} %copy-done.18) | copy-start | bytes 294916
  495.2 17.5 %copy-start.123 = (bf16[8,2048,128]{1,2,0:T(8,128)(2,1)S(1)}, bf16[8,2048,128]{1,2,0:T(8,128)(2,1)}, u32[]{:S(2)}) copy-start(bf16[8,2048,128]{1,2,0:T(8,128)(2,1)} %get-tuple-element.109) | copy-start | bytes 12582916
  501.7 19.3 %collective-permute-start.4 = (bf16[3,64,256]{2,1,0:T(8,128)(2,1)S(1)}, bf16[3,64,256]{2,1,0:T(8,128)(2,1)S(1)}, u32[]{:S(2)}, u32[]{:S(2)}) collective-permute-start(bf16[3,64,256]{2,1,0:T(8,128)(2,1)S(1)} %get-tuple-element.258), channel_id=1, source_target_pairs={{0,16},{16,32},{32,48},{48,64},{64,80},{80,96},{96,112},{1,17},{17... | collective-permute-start | bytes 294920 | tf_op jit(solution)/shard_map/ppermute | solution.py:19
  504.6 8.1 copy-start.9
  504.6 8.1 copy-start.122
  504.6 16.4 %collective-permute-start.5 = (bf16[3,64,256]{2,1,0:T(8,128)(2,1)S(1)}, bf16[3,64,256]{2,1,0:T(8,128)(2,1)S(1)}, u32[]{:S(2)}, u32[]{:S(2)}) collective-permute-start(bf16[3,64,256]{2,1,0:T(8,128)(2,1)S(1)} %get-tuple-element.259), channel_id=1, source_target_pairs={{16,0},{32,16},{48,32},{64,48},{80,64},{96,80},{112,96},{17,1},{33... | collective-permute-start | bytes 294920 | tf_op jit(solution)/shard_map/ppermute | solution.py:20
  521.0 8.3 copy-start.21
  521.0 8.3 copy-start.23
  521.7 17.1 %collective-permute-start.6 = (bf16[38,3,256]{2,1,0:T(4,128)(2,1)}, bf16[38,3,256]{2,1,0:T(4,128)(2,1)}, u32[]{:S(2)}, u32[]{:S(2)}) collective-permute-start(bf16[38,3,256]{2,1,0:T(4,128)(2,1)} %get-tuple-element.252), channel_id=1, source_target_pairs={{1,0},{2,1},{3,2},{4,3},{5,4},{6,5},{7,6},{8,7},{9,8},{10,9},{11,1... | collective-permute-start | bytes 175112 | tf_op jit(solution)/shard_map/ppermute | solution.py:20
  523.0 6.2 copy-start.110
  523.0 6.2 copy-start.111
  523.1 6.2 copy-start.112
  523.1 6.2 copy-start.113
  523.1 6.2 copy-start.114
  523.1 6.2 copy-start.115
  523.1 6.2 copy-start.116
  523.1 6.2 copy-start.117
  523.1 6.2 copy-start.118
  523.1 15.7 %collective-permute-start.7 = (bf16[38,3,256]{2,1,0:T(4,128)(2,1)}, bf16[38,3,256]{2,1,0:T(4,128)(2,1)}, u32[]{:S(2)}, u32[]{:S(2)}) collective-permute-start(bf16[38,3,256]{2,1,0:T(4,128)(2,1)} %get-tuple-element.253), channel_id=1, source_target_pairs={{0,1},{1,2},{2,3},{3,4},{4,5},{5,6},{6,7},{7,8},{8,9},{9,10},{10,1... | collective-permute-start | bytes 175112 | tf_op jit(solution)/shard_map/ppermute | solution.py:19
  540.9 21.4 %copy-start.14 = (bf16[2048,48]{0,1:T(8,128)(2,1)S(1)}, bf16[2048,48]{0,1:T(8,128)(2,1)}, u32[]{:S(2)}) copy-start(bf16[2048,48]{0,1:T(8,128)(2,1)} %copy-done.13) | copy-start | bytes 589828
  563.3 181.1 %all-reduce.14.cloned.1.call-start = ((), (), s32[]{:S(2)}) async-start(), calls=%async_computation.2 | async-start | bytes 6291456 | tf_op jit(solution)/shard_map/psum | solution.py:197
  564.7 239.0 %all-reduce.16.cloned.1.call-start = ((), (), s32[]{:S(2)}) async-start(), calls=%async_computation.3 | async-start | bytes 217088 | tf_op jit(solution)/shard_map/psum | solution.py:196
  644.4 229.6 %all-reduce.18.cloned.1.call-start = ((), (), s32[]{:S(2)}) async-start(), calls=%async_computation.4 | async-start | bytes 6291456 | tf_op jit(solution)/shard_map/psum | solution.py:196
  (73 other events, 187.8 us)
Sparse Core Ops, SparseCore 0:
  200.7 144.7 all-reduce.9
  563.4 80.8 all-reduce.11
  648.4 95.9 all-reduce.13
  746.8 56.8 all-reduce.15
  806.2 67.7 all-reduce.17
